TPU v7x, 32 devices: a whole 2x2x4 slice. The times are simulated.
32 devices in a mesh: blk: 16 (over z, x, core), sub: 2 (over y).
Axes of the slice: x: 2, y: 2, z: 4, core: 2. Of those that a mesh axis runs over, the one named last changes fastest.
Arguments:
- vectors: bfloat16 [16, 131072], P('sub', 'blk')
- energies: float32 [131072], P('blk'), may hold values from 1 to 4
- tile_values: bfloat16 [16, 128, 128, 128], P('blk', 'sub'), may hold values from -0.1875 to 0.1875
- tile_rows: int32 [16, 128], P('blk', 'sub'), may hold values from 0 to 63
- tile_cols: int32 [16, 128], P('blk', 'sub'), may hold values from 0 to 63
- tile_offsets: int32 [16, 128], P('blk', 'sub'), may hold values from 0 to 2, as said below
- tile_count: int32 [16, 2], P('blk', 'sub'), may hold values from 8 to 64, as said below
Outputs:
- residual: float32 [16, 131072], P('sub', 'blk')
Inputs may be any that keep to these rules, and one draw needn't show every extreme that they name: `tile_offsets`: an offset never exceeds the row block's index b; where the offset is 0, tile_rows >= tile_cols. `tile_count`: each count is 64 divided by 1, 2, 4 or 8.
All inputs are finite; a program needn't handle non-finite values.
Results may differ from a plain program's by a relative error of at most 0.0003.
Values may be sent and summed in bfloat16 or wider, within the bound.
No kernel may reach another device: no remote copies, remote signals or barrier semaphores. Data moves between devices by JAX's collectives and lax.ppermute only.
A program may use at most 64 MiB of HBM per device.

v0:
```python
import jax
import jax.numpy as jnp
from jax import lax
from jax.sharding import PartitionSpec as P

BW = 2


def from_behind(value, axis, steps):
    count = lax.axis_size(axis)
    first, last = (max(0, -steps), min(count, count - steps))
    return lax.ppermute(value, axis, [(source, source + steps) for source in range(first, last)])


def ritz_coefficients(gram, projected):
    lower = jnp.linalg.cholesky(gram)
    half = lax.linalg.triangular_solve(lower, projected, left_side=True, lower=True)
    return lax.linalg.triangular_solve(lower, half, left_side=True, lower=True, transpose_a=True)


def tile_products(tile_vals, row_ids, col_ids, offset_ids, live, stacked, own_block):
    width, rows_dev = own_block.shape
    tile_side = tile_vals.shape[-1]
    row_tiles = rows_dev // tile_side
    depth = stacked.shape[0]
    highest = lax.Precision.HIGHEST
    grid_view = stacked.reshape(depth, width, row_tiles, tile_side)
    sources = grid_view[offset_ids, :, col_ids, :]
    direct_terms = jnp.einsum(
        "tij,tcj->tci", tile_vals, sources, preferred_element_type=jnp.float32
    )
    own_tiles = own_block.reshape(width, row_tiles, tile_side)[:, row_ids, :]
    mirror_terms = jnp.einsum(
        "tji,ctj->tci", tile_vals, own_tiles, preferred_element_type=jnp.float32
    )
    tile_range = jnp.arange(row_tiles, dtype=jnp.int32)
    row_hot = (row_ids[:, None] == tile_range[None, :]).astype(jnp.float32) * live[:, None]
    col_hot = (col_ids[:, None] == tile_range[None, :]).astype(jnp.float32) * live[:, None]
    depth_hot = (offset_ids[:, None] == jnp.arange(depth, dtype=jnp.int32)[None, :]).astype(
        jnp.float32
    )
    direct = jnp.einsum("tci,tr->cri", direct_terms, row_hot, precision=highest).reshape(
        width, rows_dev
    )
    mirror = jnp.einsum("tci,tk,tr->kcri", mirror_terms, depth_hot, col_hot, precision=highest)
    return (direct, mirror.reshape(depth, width, rows_dev))


def send_back(pieces):
    gathered_sum = pieces[0]
    for offset in range(1, BW + 1):
        gathered_sum = gathered_sum + from_behind(pieces[offset], "blk", -offset)
    return gathered_sum


def on_device(vectors, energies, tile_values, tile_rows, tile_cols, tile_offsets, tile_count):
    columns = vectors.shape[0]
    part_index = lax.axis_index("sub")
    tile_vals = tile_values[0]
    row_ids = tile_rows[0]
    col_ids = tile_cols[0]
    offset_ids = tile_offsets[0]
    live_count = tile_count[0, 0]
    slots = tile_vals.shape[0]
    whole = lax.all_gather(vectors, "sub", axis=0, tiled=True)
    lowered = [whole]
    for offset in range(1, BW + 1):
        lowered.append(from_behind(whole, "blk", offset))
    stacked = jnp.stack(lowered, 0)
    own_block = stacked[0]
    width, rows_dev = own_block.shape
    live = (jnp.arange(slots, dtype=jnp.int32) < live_count).astype(jnp.float32)
    direct, mirror = tile_products(
        tile_vals, row_ids, col_ids, offset_ids, live, stacked, own_block
    )
    mirror = mirror.at[0].add(direct)
    applied = lax.psum_scatter(send_back(mirror), "sub", scatter_dimension=0, tiled=True)
    applied = applied + energies[None, :] * vectors.astype(jnp.float32)
    highest = lax.Precision.HIGHEST
    own_wide = own_block.astype(jnp.float32)
    gram_part = jnp.dot(own_block, vectors.T, preferred_element_type=jnp.float32)
    proj_part = jnp.dot(own_wide, applied.T, precision=highest)
    empty = jnp.zeros((width, width), jnp.float32)
    gram_full = lax.dynamic_update_slice(empty, gram_part, (0, part_index * columns))
    proj_full = lax.dynamic_update_slice(empty, proj_part, (0, part_index * columns))
    gram, projected = lax.psum((gram_full, proj_full), ("blk", "sub"))
    coefficients = ritz_coefficients(gram, projected)
    mine = lax.dynamic_slice_in_dim(coefficients, part_index * columns, columns, 1)
    return applied - jnp.dot(mine.T, own_wide, precision=highest)


def solution(mesh):
    in_specs = (
        P("sub", "blk"),
        P("blk"),
        P("blk", "sub", None, None),
        P("blk", "sub"),
        P("blk", "sub"),
        P("blk", "sub"),
        P("blk", "sub"),
    )
    out_specs = P("sub", "blk")
    return jax.shard_map(
        on_device, mesh=mesh, in_specs=in_specs, out_specs=out_specs, check_vma=False
    )
```

profile of v0, /device:TPU:0, one launch (start us, length us, event | category | flops | bytes accessed | tf_op | source)
XLA Modules:
  0.0 120.7 jit_solution(16180372393465413950)
XLA Ops:
  6.5 7.5 %all_gather.3 = bf16[16,8192]{1,0:T(8,128)(2,1)S(1)} all-gather(bf16[8,8192]{1,0:T(8,128)(2,1)} %param.9), channel_id=1, replica_groups=mesh['blk'=16,'sub'=2] {'sub'}, dimensions={0}, use_global_device_ids=true | all-gather | bytes 393216 | tf_op jit(solution)/shard_map/all_gather | solution.py:65
  14.1 3.6 %collective-permute-start.1 = (bf16[16,8192]{1,0:T(8,128)(2,1)S(1)}, bf16[16,8192]{1,0:T(8,128)(2,1)S(1)}, u32[]{:S(2)}, u32[]{:S(2)}) collective-permute-start(bf16[16,8192]{1,0:T(8,128)(2,1)S(1)} %all_gather.3), channel_id=1, source_target_pairs={{0,4},{2,6},{4,8},{6,10},{8,12},{10,14},{12,16},{14,18},{16,20},{1... | collective-permute-start | bytes 786440 | tf_op jit(solution)/shard_map/ppermute | solution.py:12
  17.6 1.3 %collective-permute-start = (bf16[16,8192]{1,0:T(8,128)(2,1)S(1)}, bf16[16,8192]{1,0:T(8,128)(2,1)S(1)}, u32[]{:S(2)}, u32[]{:S(2)}) collective-permute-start(bf16[16,8192]{1,0:T(8,128)(2,1)S(1)} %all_gather.3), channel_id=1, source_target_pairs={{0,2},{2,4},{4,6},{6,8},{8,10},{10,12},{12,14},{14,16},{16,18},{18... | collective-permute-start | bytes 786440 | tf_op jit(solution)/shard_map/ppermute | solution.py:12
  19.0 0.7 fusion.30
  19.7 0.7 fusion.29
  21.6 0.7 fusion.2
  22.3 1.4 %convolution_bitcast_fusion = f32[3,16,64,128]{3,2,1,0:T(8,128)S(1)} fusion(f32[64,16,128]{2,1,0:T(8,128)S(1)} %fusion.2, f32[64,3]{0,1:T(4,128)S(1)} %fusion.29, f32[64,64]{0,1:T(8,128)S(1)} %fusion.18), kind=kOutput, calls=%fused_computation.7 | convolution fusion | flops 302002176 | bytes 2114304 | tf_op jit(solution)/shard_map/tci,tk,tr->kcri/dot_general | solution.py:45
  23.9 1.1 copy.43
  25.1 1.3 %collective-permute-start.3 = (f32[16,8192]{1,0:T(8,128)}, f32[16,8192]{1,0:T(8,128)}, u32[]{:S(2)}, u32[]{:S(2)}) collective-permute-start(f32[16,8192]{1,0:T(8,128)} %bitcast.93), channel_id=1, source_target_pairs={{4,0},{6,2},{8,4},{10,6},{12,8},{14,10},{16,12},{18,14},{20,16},{2... | collective-permute-start | bytes 1572872 | tf_op jit(solution)/shard_map/ppermute | solution.py:12
  26.3 1.1 copy.44
  27.5 1.3 %collective-permute-start.2 = (f32[16,8192]{1,0:T(8,128)}, f32[16,8192]{1,0:T(8,128)}, u32[]{:S(2)}, u32[]{:S(2)}) collective-permute-start(f32[16,8192]{1,0:T(8,128)} %bitcast.94), channel_id=1, source_target_pairs={{2,0},{4,2},{6,4},{8,6},{10,8},{12,10},{14,12},{16,14},{18,16},{20... | collective-permute-start | bytes 1572872 | tf_op jit(solution)/shard_map/ppermute | solution.py:12
  29.5 1.0 pad_maximum_fusion
  30.5 1.9 %gather_fusion.1 = bf16[64,16,128]{2,1,0:T(8,128)(2,1)S(1)} fusion(bf16[3,16,64,128]{3,1,2,0:T(8,128)(2,1)} %pad_maximum_fusion, s32[64]{0:T(128)S(1)} %fusion.36), kind=kCustom, calls=%fused_computation.1 | custom fusion | bytes 524800 | tf_op jit(solution)/shard_map/gather | solution.py:28
  32.4 1.2 fusion
  33.6 0.7 fusion.7
  34.3 6.7 %collective-permute-done.3 = f32[16,8192]{1,0:T(8,128)} collective-permute-done((f32[16,8192]{1,0:T(8,128)}, f32[16,8192]{1,0:T(8,128)}, u32[]{:S(2)}, u32[]{:S(2)}) %collective-permute-start.3) | collective-permute-done | bytes 524320 | tf_op jit(solution)/shard_map/ppermute | solution.py:12
  41.0 2.6 %fusion.5 = f32[16,8192]{1,0:T(8,128)} fusion(f32[16,8192]{1,0:T(8,128)} %collective-permute-done.3, f32[16,8192]{1,0:T(8,128)} %collective-permute-done.2, f32[2,8,64,128]{3,2,1,0:T(8,128)S(1)} %bitcast.97, f32[2,8,64,128]{3,2,1,0:T(8,128)S(1)} %bitcast.98), kind=kLoop, calls=%fused_computation.14 | loop fusion | flops 393216 | bytes 2621440 | tf_op jit(solution)/shard_map/add | solution.py:52
  44.1 22.2 %reduce-scatter.2.cloned.1.call-done = f32[8,8192]{1,0:T(8,128)} async-done(((f32[16,8192]{1,0:T(8,128)}), f32[8,8192]{1,0:T(8,128)}) %reduce-scatter.2.cloned.1.call-update) | async-done | bytes 262160 | tf_op jit(solution)/shard_map/reduce_scatter | solution.py:77
  66.3 1.4 %convolution_bitcast_fusion.1 = f32[16,8]{1,0:T(8,128)S(1)} fusion(bf16[16,8192]{1,0:T(8,128)(2,1)S(1)} %all_gather.3, f32[8,8192]{1,0:T(8,128)} %reduce-scatter.2.cloned.1.call-done, bf16[8,8192]{1,0:T(8,128)(2,1)S(1)} %copy-done.1, f32[8192]{0:T(1024)S(1)} %copy-done.2), kind=kOutput, calls=%fused_computation.8 | convolution fusion | flops 12779520 | bytes 688640 | tf_op jit(solution)/shard_map/dot_general | solution.py:82
  67.9 39.5 %all-reduce = (f32[16,16]{1,0:T(8,128)S(1)}, f32[16,16]{1,0:T(8,128)S(1)}) all-reduce(f32[16,16]{1,0:T(8,128)S(1)} %dynamic_update_slice.7, f32[16,16]{1,0:T(8,128)S(1)} %dynamic_update_slice.6), channel_id=1, replica_groups=mesh['blk'=16,'sub'=2] {'blk','sub'}, use_global_device_ids=true, to_apply=%region_4.5 | all-reduce | flops 512 | bytes 4096 | tf_op jit(solution)/shard_map/psum | solution.py:86
  107.5 1.5 %cholesky.15 = f32[16,16]{1,0:T(8,128)S(1)} custom-call(f32[16,16]{1,0:T(8,128)S(1)} %fusion.27), custom_call_target="Cholesky" | custom-call | tf_op jit(solution)/shard_map/jit(cholesky)/cholesky | solution.py:16
  109.6 0.6 fusion.22
  110.3 1.2 %custom-call.8 = f32[1,16,16]{1,2,0:T(8,128)S(1)} custom-call(f32[1,16,16]{2,1,0:T(8,128)S(1)} %fusion.22), custom_call_target="InvertDiagBlocksLowerTriangular" | custom-call | tf_op jit(solution)/shard_map/triangular_solve | solution.py:18
  111.9 1.9 %convolution_subtract_fusion = f32[8,8192]{1,0:T(8,128)} fusion(bf16[16,8192]{1,0:T(8,128)(2,1)S(1)} %all_gather.3, f32[8,8192]{1,0:T(8,128)} %reduce-scatter.2.cloned.1.call-done, bf16[8,8192]{1,0:T(8,128)(2,1)S(1)} %copy-done.1, f32[8192]{0:T(1024)S(1)} %copy-done.2, f32[16,16]{0,1:T(8,128)S(1)} %fusion.23, s32[]{:T(128)S(6)} %select_n.42), kind=kOutput, calls=%fused_computation.2 | convolution fusion | flops 12845056 | bytes 954372 | tf_op jit(solution)/shard_map/dot_general | solution.py:89
  (41 shorter events, 3.4 us)
Async XLA Ops:
  6.5 15.1 %copy-start = (bf16[1,64,128,128]{3,2,1,0:T(8,128)(2,1)S(1)}, bf16[1,64,128,128]{3,2,1,0:T(8,128)(2,1)}, u32[]{:S(2)}) copy-start(bf16[1,64,128,128]{3,2,1,0:T(8,128)(2,1)} %param.11) | copy-start | bytes 6291460
  6.5 15.8 %copy-start.4 = (s32[1,64]{1,0:T(1,128)S(1)}, s32[1,64]{1,0:T(1,128)}, u32[]{:S(2)}) copy-start(s32[1,64]{1,0:T(1,128)} %param.13) | copy-start | bytes 772
  6.5 59.7 %reduce-scatter.2.cloned.1.call-start = ((), (), s32[]{:S(2)}) async-start(), calls=%async_computation.1 | async-start | bytes 786432 | tf_op jit(solution)/shard_map/reduce_scatter | solution.py:77
  14.1 14.9 %collective-permute-start.1 = (bf16[16,8192]{1,0:T(8,128)(2,1)S(1)}, bf16[16,8192]{1,0:T(8,128)(2,1)S(1)}, u32[]{:S(2)}, u32[]{:S(2)}) collective-permute-start(bf16[16,8192]{1,0:T(8,128)(2,1)S(1)} %all_gather.3), channel_id=1, source_target_pairs={{0,4},{2,6},{4,8},{6,10},{8,12},{10,14},{12,16},{14,18},{16,20},{1... | collective-permute-start | bytes 786440 | tf_op jit(solution)/shard_map/ppermute | solution.py:12
  17.6 11.6 %collective-permute-start = (bf16[16,8192]{1,0:T(8,128)(2,1)S(1)}, bf16[16,8192]{1,0:T(8,128)(2,1)S(1)}, u32[]{:S(2)}, u32[]{:S(2)}) collective-permute-start(bf16[16,8192]{1,0:T(8,128)(2,1)S(1)} %all_gather.3), channel_id=1, source_target_pairs={{0,2},{2,4},{4,6},{6,8},{8,10},{10,12},{12,14},{14,16},{16,18},{18... | collective-permute-start | bytes 786440 | tf_op jit(solution)/shard_map/ppermute | solution.py:12
  23.9 5.1 %copy-start.5 = (s32[1,64]{1,0:T(1,128)S(1)}, s32[1,64]{1,0:T(1,128)}, u32[]{:S(2)}) copy-start(s32[1,64]{1,0:T(1,128)} %param.14) | copy-start | bytes 772
  25.1 16.0 %collective-permute-start.3 = (f32[16,8192]{1,0:T(8,128)}, f32[16,8192]{1,0:T(8,128)}, u32[]{:S(2)}, u32[]{:S(2)}) collective-permute-start(f32[16,8192]{1,0:T(8,128)} %bitcast.93), channel_id=1, source_target_pairs={{4,0},{6,2},{8,4},{10,6},{12,8},{14,10},{16,12},{18,14},{20,16},{2... | collective-permute-start | bytes 1572872 | tf_op jit(solution)/shard_map/ppermute | solution.py:12
  27.5 13.6 %collective-permute-start.2 = (f32[16,8192]{1,0:T(8,128)}, f32[16,8192]{1,0:T(8,128)}, u32[]{:S(2)}, u32[]{:S(2)}) collective-permute-start(f32[16,8192]{1,0:T(8,128)} %bitcast.94), channel_id=1, source_target_pairs={{2,0},{4,2},{6,4},{8,6},{10,8},{12,10},{14,12},{16,14},{18,16},{20... | collective-permute-start | bytes 1572872 | tf_op jit(solution)/shard_map/ppermute | solution.py:12
  30.5 3.1 %copy-start.3 = (s32[1,64]{1,0:T(1,128)S(1)}, s32[1,64]{1,0:T(1,128)}, u32[]{:S(2)}) copy-start(s32[1,64]{1,0:T(1,128)} %param.12) | copy-start | bytes 772
  33.6 10.1 %copy-start.1 = (bf16[8,8192]{1,0:T(8,128)(2,1)S(1)}, bf16[8,8192]{1,0:T(8,128)(2,1)}, u32[]{:S(2)}) copy-start(bf16[8,8192]{1,0:T(8,128)(2,1)} %param.9) | copy-start | bytes 393220
  33.6 32.7 %copy-start.2 = (f32[8192]{0:T(1024)S(1)}, f32[8192]{0:T(1024)}, u32[]{:S(2)}) copy-start(f32[8192]{0:T(1024)} %param.10) | copy-start | bytes 98308
Sparse Core Ops, SparseCore 0:
  43.8 22.4 reduce-scatter.1
where the time goes:
time: 121 us
  blocking collectives  47 us (39%)
  waiting for transfers between devices  28.9 us (24%)
  between operations  14.3 us (12%)
  other arithmetic  8.95 us (7%)
  matrix products  7.91 us (7%)
  starting transfers between devices  7.45 us (6%)
  local copies, waits for them, and re-layouts  6.14 us (5%)
    psum x1, blocking collectives, on_device(): gram, projected = lax.psum((gram_full, proj_full), ('blk', 'sub'))  39.5 us
    reduce_scatter x1, waiting for transfers between devices, on_device(): lax.psum_scatter(send_back(mirror), 'sub', scatter_dimension=0, tiled=True)  22.2 us
    all_gather x1, blocking collectives, on_device(): whole = lax.all_gather(vectors, 'sub', axis=0, tiled=True)  7.51 us
    ppermute x4, starting transfers between devices, from_behind(): lax.ppermute(value, axis, [(source, source + steps) for source in range(f...  7.45 us
    ppermute x4, waiting for transfers between devices, from_behind(): lax.ppermute(value, axis, [(source, source + steps) for source in range(f...  6.71 us
    add x1, other arithmetic, send_back(): gathered_sum = gathered_sum + from_behind(pieces[offset], 'blk', -offset)  2.61 us
  transfers between devices with their start and end apart: 5, of which 2 were waited for; matrix products, arithmetic and copies ran while one was open for 10% of the time, Pallas kernels for 0%

commit v1 on v0

--- a/solution.py
+++ b/solution.py
@@ -62,7 +62,9 @@
     offset_ids = tile_offsets[0]
     live_count = tile_count[0, 0]
     slots = tile_vals.shape[0]
-    whole = lax.all_gather(vectors, "sub", axis=0, tiled=True)
+    whole = jnp.concatenate(
+        lax.all_to_all(jnp.stack([vectors] * lax.axis_size("sub")), "sub", 0, 0), axis=0
+    )
     lowered = [whole]
     for offset in range(1, BW + 1):
         lowered.append(from_behind(whole, "blk", offset))

time: 121 us -> 123 us (1.017)
  blocking collectives: 47 us -> 39.6 us
  starting transfers between devices: 7.45 us -> 13.1 us
  other arithmetic: 8.95 us -> 12.1 us
  local copies, waits for them, and re-layouts: 6.14 us -> 8.14 us
  waiting for transfers between devices: 28.9 us -> 27.4 us
    all_gather x1 -> x0, blocking collectives: 7.51 us -> none  [on_device(): whole = lax.all_gather(vectors, 'sub', axis=0, tiled=True)]
    all_to_all x0 -> x1, starting transfers between devices: none -> 4.23 us  [on_device(): lax.all_to_all(jnp.stack([vectors] * lax.axis_size('sub')), 'sub', 0, 0)]
    reduce_scatter x1, waiting for transfers between devices: 22.2 us -> 18.9 us  [on_device(): lax.psum_scatter(send_back(mirror), 'sub', scatter_dimension=0, tiled=True)]
    all_to_all x0 -> x1, waiting for transfers between devices: none -> 2.54 us  [on_device(): lax.all_to_all(jnp.stack([vectors] * lax.axis_size('sub')), 'sub', 0, 0)]
    unnamed x17 -> x13, local copies, waits for them, and re-layouts: 2.4 us -> 4.29 us
    another operation x1 -> x2, other arithmetic: 0.66 us -> 2.5 us  [the longest x1 1.84 us: on_device(): jnp.stack([vectors] * lax.axis_size('sub'))]
    ppermute x4, starting transfers between devices: 7.45 us -> 8.84 us  [from_behind(): lax.ppermute(value, axis, [(source, source + steps) for source in range(f...]
  transfers between devices with their start and end apart: 5 -> 6, of which waited for: 2 -> 3; matrix products, arithmetic and copies ran while one was open for 10% -> 13% of each run, Pallas kernels for 0% -> 0%
where the time goes in v1:
time: 123 us; the launch traced here: 122 us
  blocking collectives  39.6 us (32%)
  waiting for transfers between devices  27.4 us (22%)
  between operations  14.2 us (12%)
  starting transfers between devices  13.1 us (11%)
  other arithmetic  12.1 us (10%)
  local copies, waits for them, and re-layouts  8.14 us (7%)
  matrix products  7.91 us (6%)
    psum x1, blocking collectives, on_device(): gram, projected = lax.psum((gram_full, proj_full), ('blk', 'sub'))  39.6 us
    reduce_scatter x1, waiting for transfers between devices, on_device(): lax.psum_scatter(send_back(mirror), 'sub', scatter_dimension=0, tiled=True)  18.9 us
    ppermute x4, starting transfers between devices, from_behind(): lax.ppermute(value, axis, [(source, source + steps) for source in range(f...  8.84 us
    ppermute x4, waiting for transfers between devices, from_behind(): lax.ppermute(value, axis, [(source, source + steps) for source in range(f...  5.87 us
    unnamed x13, local copies, waits for them, and re-layouts  4.29 us
    all_to_all x1, starting transfers between devices, on_device(): lax.all_to_all(jnp.stack([vectors] * lax.axis_size('sub')), 'sub', 0, 0)  4.23 us
    add x1, other arithmetic, send_back(): gathered_sum = gathered_sum + from_behind(pieces[offset], 'blk', -offset)  2.61 us
    all_to_all x1, waiting for transfers between devices, on_device(): lax.all_to_all(jnp.stack([vectors] * lax.axis_size('sub')), 'sub', 0, 0)  2.54 us
  transfers between devices with their start and end apart: 6, of which 3 were waited for; matrix products, arithmetic and copies ran while one was open for 13% of the time, Pallas kernels for 0%

profile of v1, /device:TPU:0, one launch (start us, length us, event | category | flops | bytes accessed | tf_op | source)
XLA Modules:
  0.0 122.4 jit_solution(16771734423919682065)
XLA Ops:
  6.5 1.8 %pad_maximum_fusion.1 = bf16[2,8,8192]{2,1,0:T(8,128)(2,1)} fusion(bf16[1,8,8192]{2,1,0:T(8,128)(2,1)} %bitcast.104), kind=kLoop, calls=%fused_computation.18 | loop fusion | flops 131072 | bytes 393216 | tf_op jit(solution)/shard_map/stack | solution.py:66
  8.4 4.2 %all-to-all-start = ((bf16[2,8,8192]{2,1,0:T(8,128)(2,1)}), bf16[2,8,8192]{2,1,0:T(8,128)(2,1)S(1)}, u32[]{:S(2)}, u32[]{:S(2)}) async-start(bf16[2,8,8192]{2,1,0:T(8,128)(2,1)} %pad_maximum_fusion.1), calls=%async_computation | async-start | bytes 524288 | tf_op jit(solution)/shard_map/all_to_all | solution.py:66
  16.0 2.5 %all-to-all-done = bf16[2,8,8192]{2,1,0:T(8,128)(2,1)S(1)} async-done(((bf16[2,8,8192]{2,1,0:T(8,128)(2,1)}), bf16[2,8,8192]{2,1,0:T(8,128)(2,1)S(1)}, u32[]{:S(2)}, u32[]{:S(2)}) %all-to-all-start) | async-done | bytes 262176 | tf_op jit(solution)/shard_map/all_to_all | solution.py:66
  18.5 4.3 %collective-permute-start.1 = (bf16[16,8192]{1,0:T(8,128)(2,1)S(1)}, bf16[16,8192]{1,0:T(8,128)(2,1)}, u32[]{:S(2)}, u32[]{:S(2)}) collective-permute-start(bf16[16,8192]{1,0:T(8,128)(2,1)S(1)} %bitcast.98), channel_id=1, source_target_pairs={{0,4},{2,6},{4,8},{6,10},{8,12},{10,14},{12,16},{14,18},{16,20},{1... | collective-permute-start | bytes 786440 | tf_op jit(solution)/shard_map/ppermute | solution.py:12
  22.8 2.0 %collective-permute-start = (bf16[16,8192]{1,0:T(8,128)(2,1)S(1)}, bf16[16,8192]{1,0:T(8,128)(2,1)}, u32[]{:S(2)}, u32[]{:S(2)}) collective-permute-start(bf16[16,8192]{1,0:T(8,128)(2,1)S(1)} %bitcast.99), channel_id=1, source_target_pairs={{0,2},{2,4},{4,6},{6,8},{8,10},{10,12},{12,14},{14,16},{16,18},{18... | collective-permute-start | bytes 786440 | tf_op jit(solution)/shard_map/ppermute | solution.py:12
  26.3 1.4 %convolution_bitcast_fusion = f32[3,16,64,128]{3,2,1,0:T(8,128)S(1)} fusion(f32[64,16,128]{2,1,0:T(8,128)S(1)} %fusion.2, f32[64,3]{0,1:T(4,128)S(1)} %fusion.30, f32[64,64]{0,1:T(8,128)S(1)} %fusion.19), kind=kOutput, calls=%fused_computation.7 | convolution fusion | flops 302002176 | bytes 2114304 | tf_op jit(solution)/shard_map/tci,tk,tr->kcri/dot_general | solution.py:45
  27.9 1.1 copy.42
  29.0 1.3 %collective-permute-start.3 = (f32[16,8192]{1,0:T(8,128)}, f32[16,8192]{1,0:T(8,128)}, u32[]{:S(2)}, u32[]{:S(2)}) collective-permute-start(f32[16,8192]{1,0:T(8,128)} %bitcast.95), channel_id=1, source_target_pairs={{4,0},{6,2},{8,4},{10,6},{12,8},{14,10},{16,12},{18,14},{20,16},{2... | collective-permute-start | bytes 1572872 | tf_op jit(solution)/shard_map/ppermute | solution.py:12
  30.3 1.1 copy.43
  31.4 1.3 %collective-permute-start.2 = (f32[16,8192]{1,0:T(8,128)}, f32[16,8192]{1,0:T(8,128)}, u32[]{:S(2)}, u32[]{:S(2)}) collective-permute-start(f32[16,8192]{1,0:T(8,128)} %bitcast.96), channel_id=1, source_target_pairs={{2,0},{4,2},{6,4},{8,6},{10,8},{12,10},{14,12},{16,14},{18,16},{20... | collective-permute-start | bytes 1572872 | tf_op jit(solution)/shard_map/ppermute | solution.py:12
  32.9 1.0 copy.28
  34.1 1.0 copy.27
  35.3 1.0 pad_maximum_fusion
  36.3 1.9 %gather_fusion.1 = bf16[64,16,128]{2,1,0:T(8,128)(2,1)S(1)} fusion(bf16[3,16,64,128]{3,1,2,0:T(8,128)(2,1)} %pad_maximum_fusion, s32[64]{0:T(128)S(1)} %fusion.37), kind=kCustom, calls=%fused_computation.1 | custom fusion | bytes 524800 | tf_op jit(solution)/shard_map/gather | solution.py:28
  38.2 1.2 fusion
  39.4 0.7 fusion.7
  40.1 5.9 %collective-permute-done.3 = f32[16,8192]{1,0:T(8,128)} collective-permute-done((f32[16,8192]{1,0:T(8,128)}, f32[16,8192]{1,0:T(8,128)}, u32[]{:S(2)}, u32[]{:S(2)}) %collective-permute-start.3) | collective-permute-done | bytes 524320 | tf_op jit(solution)/shard_map/ppermute | solution.py:12
  46.0 2.6 %fusion.5 = f32[16,8192]{1,0:T(8,128)} fusion(f32[16,8192]{1,0:T(8,128)} %collective-permute-done.3, f32[16,8192]{1,0:T(8,128)} %collective-permute-done.2, f32[2,8,64,128]{3,2,1,0:T(8,128)S(1)} %bitcast.103, f32[2,8,64,128]{3,2,1,0:T(8,128)S(1)} %bitcast.105), kind=kLoop, calls=%fused_computation.13 | loop fusion | flops 393216 | bytes 2621440 | tf_op jit(solution)/shard_map/add | solution.py:52
  49.0 18.9 %reduce-scatter.2.cloned.1.call-done = f32[8,8192]{1,0:T(8,128)} async-done(((f32[16,8192]{1,0:T(8,128)}), f32[8,8192]{1,0:T(8,128)}) %reduce-scatter.2.cloned.1.call-update) | async-done | bytes 262160 | tf_op jit(solution)/shard_map/reduce_scatter | solution.py:79
  68.0 1.4 %fusion.11 = f32[16,8]{1,0:T(8,128)S(1)} fusion(f32[8,8192]{1,0:T(8,128)} %reduce-scatter.2.cloned.1.call-done, bf16[8,8192]{1,0:T(8,128)(2,1)S(1)} %copy-done.1, f32[8192]{0:T(1024)S(1)} %copy-done.2, bf16[2,8,8192]{2,1,0:T(8,128)(2,1)S(1)} %all-to-all-done), kind=kOutput, calls=%fused_computation.21 | convolution fusion | flops 12779520 | bytes 688640 | tf_op jit(solution)/shard_map/dot_general | solution.py:84
  69.6 39.6 %all-reduce = (f32[16,16]{1,0:T(8,128)S(1)}, f32[16,16]{1,0:T(8,128)S(1)}) all-reduce(f32[16,16]{1,0:T(8,128)S(1)} %dynamic_update_slice.7, f32[16,16]{1,0:T(8,128)S(1)} %dynamic_update_slice.6), channel_id=1, replica_groups=mesh['blk'=16,'sub'=2] {'blk','sub'}, use_global_device_ids=true, to_apply=%region_4.5 | all-reduce | flops 512 | bytes 4096 | tf_op jit(solution)/shard_map/psum | solution.py:88
  109.2 1.5 %cholesky.15 = f32[16,16]{1,0:T(8,128)S(1)} custom-call(f32[16,16]{1,0:T(8,128)S(1)} %fusion.28), custom_call_target="Cholesky" | custom-call | tf_op jit(solution)/shard_map/jit(cholesky)/cholesky | solution.py:16
  112.0 1.2 %custom-call.8 = f32[1,16,16]{1,2,0:T(8,128)S(1)} custom-call(f32[1,16,16]{2,1,0:T(8,128)S(1)} %fusion.23), custom_call_target="InvertDiagBlocksLowerTriangular" | custom-call | tf_op jit(solution)/shard_map/triangular_solve | solution.py:18
  113.6 1.9 %convolution_subtract_fusion = f32[8,8192]{1,0:T(8,128)} fusion(f32[8,8192]{1,0:T(8,128)} %reduce-scatter.2.cloned.1.call-done, bf16[8,8192]{1,0:T(8,128)(2,1)S(1)} %copy-done.1, f32[8192]{0:T(1024)S(1)} %copy-done.2, f32[16,16]{0,1:T(8,128)S(1)} %fusion.24, s32[]{:T(128)S(6)} %select_n.42, bf16[2,8,8192]{2,1,0:T(8,128)(2,1)S(1)} %all-to-all-done), kind=kOutput, calls=%fused_computation.2 | convolution fusion | flops 12845056 | bytes 954372 | tf_op jit(solution)/shard_map/dot_general | solution.py:91
  (39 shorter events, 7.3 us)
Async XLA Ops:
  6.5 19.1 %copy-start = (bf16[1,64,128,128]{3,2,1,0:T(8,128)(2,1)S(1)}, bf16[1,64,128,128]{3,2,1,0:T(8,128)(2,1)}, u32[]{:S(2)}) copy-start(bf16[1,64,128,128]{3,2,1,0:T(8,128)(2,1)} %param.11) | copy-start | bytes 6291460
  8.4 10.1 %all-to-all-start = ((bf16[2,8,8192]{2,1,0:T(8,128)(2,1)}), bf16[2,8,8192]{2,1,0:T(8,128)(2,1)S(1)}, u32[]{:S(2)}, u32[]{:S(2)}) async-start(bf16[2,8,8192]{2,1,0:T(8,128)(2,1)} %pad_maximum_fusion.1), calls=%async_computation | async-start | bytes 524288 | tf_op jit(solution)/shard_map/all_to_all | solution.py:66
  12.6 55.3 %reduce-scatter.2.cloned.1.call-start = ((), (), s32[]{:S(2)}) async-start(), calls=%async_computation.2 | async-start | bytes 786432 | tf_op jit(solution)/shard_map/reduce_scatter | solution.py:79
  18.5 14.4 %collective-permute-start.1 = (bf16[16,8192]{1,0:T(8,128)(2,1)S(1)}, bf16[16,8192]{1,0:T(8,128)(2,1)}, u32[]{:S(2)}, u32[]{:S(2)}) collective-permute-start(bf16[16,8192]{1,0:T(8,128)(2,1)S(1)} %bitcast.98), channel_id=1, source_target_pairs={{0,4},{2,6},{4,8},{6,10},{8,12},{10,14},{12,16},{14,18},{16,20},{1... | collective-permute-start | bytes 786440 | tf_op jit(solution)/shard_map/ppermute | solution.py:12
  22.8 11.3 %collective-permute-start = (bf16[16,8192]{1,0:T(8,128)(2,1)S(1)}, bf16[16,8192]{1,0:T(8,128)(2,1)}, u32[]{:S(2)}, u32[]{:S(2)}) collective-permute-start(bf16[16,8192]{1,0:T(8,128)(2,1)S(1)} %bitcast.99), channel_id=1, source_target_pairs={{0,2},{2,4},{4,6},{6,8},{8,10},{10,12},{12,14},{14,16},{16,18},{18... | collective-permute-start | bytes 786440 | tf_op jit(solution)/shard_map/ppermute | solution.py:12
  29.0 16.9 %collective-permute-start.3 = (f32[16,8192]{1,0:T(8,128)}, f32[16,8192]{1,0:T(8,128)}, u32[]{:S(2)}, u32[]{:S(2)}) collective-permute-start(f32[16,8192]{1,0:T(8,128)} %bitcast.95), channel_id=1, source_target_pairs={{4,0},{6,2},{8,4},{10,6},{12,8},{14,10},{16,12},{18,14},{20,16},{2... | collective-permute-start | bytes 1572872 | tf_op jit(solution)/shard_map/ppermute | solution.py:12
  31.4 14.6 %collective-permute-start.2 = (f32[16,8192]{1,0:T(8,128)}, f32[16,8192]{1,0:T(8,128)}, u32[]{:S(2)}, u32[]{:S(2)}) collective-permute-start(f32[16,8192]{1,0:T(8,128)} %bitcast.96), channel_id=1, source_target_pairs={{2,0},{4,2},{6,4},{8,6},{10,8},{12,10},{14,12},{16,14},{18,16},{20... | collective-permute-start | bytes 1572872 | tf_op jit(solution)/shard_map/ppermute | solution.py:12
  36.3 3.1 %copy-start.3 = (s32[1,64]{1,0:T(1,128)S(1)}, s32[1,64]{1,0:T(1,128)}, u32[]{:S(2)}) copy-start(s32[1,64]{1,0:T(1,128)} %param.12) | copy-start | bytes 772
  39.4 9.3 %copy-start.1 = (bf16[8,8192]{1,0:T(8,128)(2,1)S(1)}, bf16[8,8192]{1,0:T(8,128)(2,1)}, u32[]{:S(2)}) copy-start(bf16[8,8192]{1,0:T(8,128)(2,1)} %param.9) | copy-start | bytes 393220
  39.4 28.6 %copy-start.2 = (f32[8192]{0:T(1024)S(1)}, f32[8192]{0:T(1024)}, u32[]{:S(2)}) copy-start(f32[8192]{0:T(1024)} %param.10) | copy-start | bytes 98308
Sparse Core Ops, SparseCore 0:
  48.7 19.1 reduce-scatter.1
